TPU v7x, 128 devices: a whole 4x4x4 slice. The times are simulated.
128 devices in a mesh: tm: 32 (over y, z, core), space: 4 (over x).
Axes of the slice: x: 4, y: 4, z: 4, core: 2. Of those that a mesh axis runs over, the one named last changes fastest.
Arguments:
- scenes: float32 [32, 4096, 2048], P('tm', None, 'space'), may hold values from -6 to 6
- offset_y: int32 [32], replicated, may hold values from -2048 to 2048
- offset_x: int32 [32], replicated, may hold values from -63 to 63
- frac_y: float32 [32], replicated, may hold values from 0.05 to 0.95
- frac_x: float32 [32], replicated, may hold values from 0.05 to 0.95
Outputs:
- warped: float32 [32, 4096, 2048], P(None, 'tm', 'space')
All inputs are finite; a program needn't handle non-finite values.
Results may differ from a plain program's by a relative error of at most 0.0003.
Values sent between devices are 32-bit elements; how exact they have to be, the bound alone decides.
A program may use at most 128 MiB of HBM per device.

v0:
```python
import jax
import jax.numpy as jnp
from jax import lax
from jax.sharding import PartitionSpec as P

HALO = 64


def with_halo(block, sides, width):
    for axis, dim in sides:
        count = lax.axis_size(axis)
        forward = [(i, i + 1) for i in range(count - 1)]
        backward = [(target, source) for source, target in forward]
        low = lax.ppermute(
            lax.slice_in_dim(block, block.shape[dim] - width, None, axis=dim), axis, forward
        )
        high = lax.ppermute(lax.slice_in_dim(block, 0, width, axis=dim), axis, backward)
        block = jnp.concatenate([low, block, high], axis=dim)
    return block


def warp_columns(extended, offset, fraction):
    width_cols = extended.shape[-1] - 2 * HALO

    def blend_scene(picture, shift_col, weight_col):
        last_axis = picture.ndim - 1
        before_pixel = lax.dynamic_slice_in_dim(
            picture, HALO - shift_col - 1, width_cols, last_axis
        )
        at_pixel = lax.dynamic_slice_in_dim(picture, HALO - shift_col, width_cols, last_axis)
        return weight_col * before_pixel + (1.0 - weight_col) * at_pixel

    return jax.vmap(blend_scene)(extended, offset, fraction)


def warp_rows(image, offset, fraction, block_total):
    scene_count, grid_rows, width_cols = image.shape
    margin = grid_rows // 2 + 2
    padded = jnp.pad(image, ((0, 0), (margin, margin), (0, 0)))

    def blend_scene(picture, shift_row, weight_row):
        window = lax.dynamic_slice_in_dim(picture, margin - shift_row - 1, grid_rows + 1, 0)
        return weight_row * window[:grid_rows] + (1.0 - weight_row) * window[1:]

    result = jax.vmap(blend_scene)(padded, offset, fraction)
    return result.reshape(scene_count, block_total, grid_rows // block_total, width_cols)


def body(scenes, offset_y, offset_x, frac_y, frac_x):
    local_count = scenes.shape[0]
    first_scene = lax.axis_index("tm") * local_count
    block_total = lax.axis_size("tm")

    def local_part(values):
        return lax.dynamic_slice_in_dim(values, first_scene, local_count)

    extended = with_halo(scenes, (("space", 2),), HALO)
    col_warped = warp_columns(extended, local_part(offset_x), local_part(frac_x))
    row_warped = warp_rows(col_warped, local_part(offset_y), local_part(frac_y), block_total)
    moved = lax.all_to_all(row_warped, "tm", split_axis=1, concat_axis=0, tiled=True)
    scene_count, block_count, pixel_rows, width_cols = moved.shape
    return moved.reshape(scene_count, block_count * pixel_rows, width_cols)


def solution(mesh):
    return jax.shard_map(
        body,
        mesh=mesh,
        in_specs=(P("tm", None, "space"), P(), P(), P(), P()),
        out_specs=P(None, "tm", "space"),
        check_vma=False,
    )
```

profile of v0, /device:TPU:1, one launch (start us, length us, event | category | flops | bytes accessed | tf_op | source)
XLA Modules:
  0.0 190.6 jit_solution(4888056139223608207)
XLA Ops:
  0.0 0.0 copy-start
  0.0 0.0 copy-start.3
  0.0 4.2 %fusion.4 = (f32[1,4096,64]{2,1,0:T(8,128)}, f32[1,4096,64]{2,1,0:T(8,128)S(1)}) fusion(f32[1,4096,512]{2,1,0:T(8,128)} %param.5), kind=kLoop, calls=%fused_computation.9 | loop fusion | bytes 4194304 | tf_op jit(solution)/shard_map/slice | solution.py:15
  4.2 2.2 %copy.10 = f32[1,4096,64]{1,2,0:T(8,128)S(1)} copy(f32[1,4096,64]{2,1,0:T(8,128)} %get-tuple-element.38) | data formatting | bytes 2097152
  6.4 5.0 %collective-permute-start = (f32[1,4096,64]{1,2,0:T(8,128)S(1)}, f32[1,4096,64]{1,2,0:T(8,128)}, u32[]{:S(2)}, u32[]{:S(2)}) collective-permute-start(f32[1,4096,64]{1,2,0:T(8,128)S(1)} %copy.10), channel_id=1, source_target_pairs={{0,1},{1,2},{2,3},{4,5},{5,6},{6,7},{8,9},{9,10},{10,11},{12,13},{... | collective-permute-start | bytes 3145736 | tf_op jit(solution)/shard_map/ppermute | solution.py:14
  11.4 1.6 copy.11
  13.0 1.3 collective-permute-start.1
  14.3 0.0 copy-done
  14.3 0.7 dynamic_slice.14
  17.7 0.0 copy-done.1
  17.7 0.6 dynamic_slice.13
  18.2 0.0 copy-done.2
  18.2 0.6 dynamic_slice.15
  20.3 0.0 copy-done.3
  20.3 0.6 dynamic_slice.12
  22.0 10.2 %collective-permute-done = f32[1,4096,64]{1,2,0:T(8,128)} collective-permute-done((f32[1,4096,64]{1,2,0:T(8,128)S(1)}, f32[1,4096,64]{1,2,0:T(8,128)}, u32[]{:S(2)}, u32[]{:S(2)}) %collective-permute-start) | collective-permute-done | bytes 1048608 | tf_op jit(solution)/shard_map/ppermute | solution.py:14
  32.2 1.8 copy.8
  34.0 4.9 %collective-permute-done.1 = f32[1,4096,64]{1,2,0:T(8,128)} collective-permute-done((f32[1,4096,64]{1,2,0:T(8,128)}, f32[1,4096,64]{1,2,0:T(8,128)}, u32[]{:S(2)}, u32[]{:S(2)}) %collective-permute-start.1) | collective-permute-done | bytes 1048608 | tf_op jit(solution)/shard_map/ppermute | solution.py:17
  38.9 3.2 %copy.9 = f32[1,4096,64]{2,1,0:T(8,128)} copy(f32[1,4096,64]{1,2,0:T(8,128)} %collective-permute-done.1) | data formatting | bytes 2097152 | tf_op jit(solution)/shard_map/ppermute | solution.py:17
  42.0 11.3 %pad_maximum_fusion = f32[1,4096,640]{2,1,0:T(8,128)} fusion(f32[1,4096,64]{2,1,0:T(8,128)} %copy.9, f32[1,4096,512]{2,1,0:T(8,128)} %param.5, f32[1,4096,64]{2,1,0:T(8,128)S(1)} %copy.8), kind=kLoop, calls=%fused_computation.2 | loop fusion | flops 5242880 | bytes 20971520 | tf_op jit(solution)/shard_map/concatenate | solution.py:18
  53.3 15.4 %fusion.3 = f32[1,4096,512]{2,1,0:T(8,128)} fusion(f32[1,4096,640]{2,1,0:T(8,128)} %pad_maximum_fusion, s32[]{:T(128)} %bitcast.4, s32[]{:T(128)} %bitcast.2, f32[]{:T(128)} %bitcast.3, f32[]{:T(128)} %bitcast.1), kind=kLoop, calls=%fused_computation.7 | loop fusion | flops 6291456 | bytes 25165840 | tf_op jit(solution)/shard_map/vmap()/add | solution.py:31
  68.7 12.6 %fusion.1 = f32[1,4096,512]{2,1,0:T(8,128)} fusion(s32[]{:T(128)S(6)} %add.50, f32[1,4096,512]{2,1,0:T(8,128)} %fusion.3, s32[]{:T(128)} %bitcast.5, f32[]{:T(128)} %bitcast.6, f32[]{:T(128)} %bitcast), kind=kLoop, calls=%fused_computation.4 | loop fusion | flops 6291456 | bytes 16777232 | tf_op jit(solution)/shard_map/vmap()/add | solution.py:43
  81.3 105.9 %all_to_all.4 = f32[1,32,128,512]{3,2,0,1:T(8,128)S(1)} all-to-all(f32[1,32,128,512]{3,2,0,1:T(8,128)} %bitcast.9), channel_id=1, replica_groups=mesh['tm'=32,'space'=4] {'tm'}, dimensions={1} | all-to-all | bytes 16777216 | tf_op jit(solution)/shard_map/all_to_all | solution.py:60
  187.2 3.4 %copy.13 = f32[32,128,512]{2,1,0:T(8,128)} copy(f32[32,128,512]{2,1,0:T(8,128)S(1)} %bitcast.10) | data formatting | bytes 16777216
  (2 shorter events, 0.0 us)
Async XLA Ops:
  0.0 14.3 %copy-start = (s32[32]{0:T(128)S(1)}, s32[32]{0:T(128)}, u32[]{:S(2)}) copy-start(s32[32]{0:T(128)} %param.7) | copy-start | bytes 388
  0.0 17.7 %copy-start.1 = (f32[32]{0:T(128)S(1)}, f32[32]{0:T(128)}, u32[]{:S(2)}) copy-start(f32[32]{0:T(128)} %param.9) | copy-start | bytes 388
  0.0 18.2 %copy-start.2 = (s32[32]{0:T(128)S(1)}, s32[32]{0:T(128)}, u32[]{:S(2)}) copy-start(s32[32]{0:T(128)} %param.6) | copy-start | bytes 388
  0.0 20.2 %copy-start.3 = (f32[32]{0:T(128)S(1)}, f32[32]{0:T(128)}, u32[]{:S(2)}) copy-start(f32[32]{0:T(128)} %param.8) | copy-start | bytes 388
  6.4 25.8 %collective-permute-start = (f32[1,4096,64]{1,2,0:T(8,128)S(1)}, f32[1,4096,64]{1,2,0:T(8,128)}, u32[]{:S(2)}, u32[]{:S(2)}) collective-permute-start(f32[1,4096,64]{1,2,0:T(8,128)S(1)} %copy.10), channel_id=1, source_target_pairs={{0,1},{1,2},{2,3},{4,5},{5,6},{6,7},{8,9},{9,10},{10,11},{12,13},{... | collective-permute-start | bytes 3145736 | tf_op jit(solution)/shard_map/ppermute | solution.py:14
  13.0 25.9 %collective-permute-start.1 = (f32[1,4096,64]{1,2,0:T(8,128)}, f32[1,4096,64]{1,2,0:T(8,128)}, u32[]{:S(2)}, u32[]{:S(2)}) collective-permute-start(f32[1,4096,64]{1,2,0:T(8,128)} %copy.11), channel_id=1, source_target_pairs={{1,0},{2,1},{3,2},{5,4},{6,5},{7,6},{9,8},{10,9},{11,10},{13,12},{... | collective-permute-start | bytes 3145736 | tf_op jit(solution)/shard_map/ppermute | solution.py:17
where the time goes:
time: 191 us
  blocking collectives  106 us (55%)
  other arithmetic  39.3 us (21%)
  local copies, waits for them, and re-layouts  18.8 us (10%)
  waiting for transfers between devices  15.1 us (8%)
  starting transfers between devices  6.27 us (3%)
  between operations  5.32 us (3%)
    all_to_all x1, blocking collectives, body(): lax.all_to_all(row_warped, 'tm', split_axis=1, concat_axis=0, tiled=True)  106 us
    add x1, other arithmetic, blend_scene(): return weight_col * before_pixel + (1.0 - weight_col) * at_pixel  15.4 us
    add x1, other arithmetic, blend_scene(): return weight_row * window[:grid_rows] + (1.0 - weight_row) * window[1:]  12.6 us
    concatenate x1, other arithmetic, with_halo(): block = jnp.concatenate([low, block, high], axis=dim)  11.3 us
    ppermute x1, waiting for transfers between devices, with_halo(): lax.ppermute(lax.slice_in_dim(block, block.shape[dim] - width, None, axis...  10.2 us
    unnamed x11, local copies, waits for them, and re-layouts  7.14 us
    ppermute x1, starting transfers between devices, with_halo(): lax.ppermute(lax.slice_in_dim(block, block.shape[dim] - width, None, axis...  4.99 us
    ppermute x1, waiting for transfers between devices, with_halo(): lax.ppermute(lax.slice_in_dim(block, 0, width, axis=dim), axis, backward)  4.87 us
  transfers between devices with their start and end apart: 2, of which 2 were waited for; matrix products, arithmetic and copies ran while one was open for 3% of the time, Pallas kernels for 0%

commit v1 on v0

v1 whole, which is shorter than its diff:
```python
import jax
import jax.numpy as jnp
from jax import lax
from jax.experimental import pallas as pl
from jax.experimental.pallas import tpu as pltpu
from jax.sharding import PartitionSpec as P

MESH = pl.DeviceIdType.MESH
LANES = 128
PAD = 136
PIECE = 32


def send_order():
    groups = (
        ((1, 0), (3, 0), (0, 1), (0, 3)),
        ((1, 1), (3, 3)),
        ((1, 3), (3, 1)),
        ((2, 0), (0, 2)),
        ((2, 1), (1, 2), (2, 3), (3, 2)),
        ((2, 2),),
    )
    order = [(dy, dz, dc) for group in groups for dc in range(2) for dy, dz in group]
    return order + [(0, 0, 1)]


ORDER = send_order()


def warp_kernel(
    oy_ref, ox_ref, fy_ref, fx_ref, scene_ref, out_ref,
    src, send, pack_out, pack_in, load_sem, send_sem, recv_sem, halo_send_sem, halo_recv_sem,
):
    rows = scene_ref.shape[1]
    tiles = scene_ref.shape[2] // LANES
    tile_rows = out_ref.shape[1]
    half = rows // 2
    me = lax.axis_index("tm")
    x = lax.axis_index("space")
    y, z, core = me // 8, (me // 2) % 4, me % 2

    def member(dy, dz, dc, sign):
        return (
            ((y + sign * dy + 4) % 4) * 8 + ((z + sign * dz + 4) % 4) * 2 + (core + dc) % 2
        )

    left, right = (x + 3) % 4, (x + 1) % 4

    barrier = pltpu.get_barrier_semaphore()
    for dy, dz, dc in ORDER:
        pl.semaphore_signal(
            barrier, inc=1, device_id=(member(dy, dz, dc, -1), x), device_id_type=MESH
        )
    for side in (left, right):
        pl.semaphore_signal(barrier, inc=1, device_id=(me, side), device_id_type=MESH)

    loads = []
    for tile in range(tiles):
        load = pltpu.make_async_copy(
            scene_ref.at[0, :, pl.ds(tile * LANES, LANES)],
            src.at[tile, pl.ds(PAD, rows)],
            load_sem.at[tile],
        )
        load.start()
        loads.append(load)
    zero_rows = jnp.zeros((PAD, LANES), jnp.float32)
    for plane in range(tiles + 1):
        src[plane, pl.ds(0, PAD)] = zero_rows
        src[plane, pl.ds(PAD + rows, PAD)] = zero_rows

    shift_y, shift_x = oy_ref[me], ox_ref[me]
    weight_y, weight_x = fy_ref[me], fx_ref[me]
    lane = lax.broadcasted_iota(jnp.int32, (PIECE, LANES), 1)
    rightward = shift_x >= 0
    low = jnp.where(rightward, 0, -shift_x)
    high = jnp.where(rightward, LANES - shift_x, LANES)
    low_before = jnp.where(rightward, 0, -shift_x - 1)
    high_before = jnp.where(rightward, LANES - 1 - shift_x, LANES)
    own_at = (lane >= low) & (lane < high)
    own_before = (lane >= low_before) & (lane < high_before)
    roll_at = (shift_x + LANES) % LANES
    roll_before = (shift_x + 1 + LANES) % LANES
    step = jnp.where(rightward, tiles, 1)

    def blend(dest, tile, part):
        base = jnp.clip(dest * tile_rows - shift_y - 1, -tile_rows - 1, rows)
        base = base + (PAD + part * PIECE)

        def blend_rows(plane):
            above = src[plane, pl.ds(base, PIECE)]
            at = src[plane, pl.ds(base + 1, PIECE)]
            return weight_y * above + (1.0 - weight_y) * at

        own = blend_rows(tile)
        beside = blend_rows((tile + step) % (tiles + 1))
        at = pltpu.roll(jnp.where(own_at, own, beside), roll_at, 1)
        before = pltpu.roll(jnp.where(own_before, own, beside), roll_before, 1)
        return weight_x * before + (1.0 - weight_x) * at

    parts = tile_rows // PIECE

    def send_piece(tile, part):
        lanes = pl.ds(pl.multiple_of(tile * LANES, LANES), LANES)
        piece = pl.ds(pl.multiple_of(part * PIECE, PIECE), PIECE)
        for slot, (dy, dz, dc) in enumerate(ORDER):
            dest = member(dy, dz, dc, 1)
            send[slot, tile, piece] = blend(dest, tile, part)
            pltpu.make_async_remote_copy(
                src_ref=send.at[slot, tile, piece],
                dst_ref=out_ref.at[me, piece, lanes],
                send_sem=send_sem.at[slot],
                recv_sem=recv_sem.at[slot],
                device_id=(dest, x),
                device_id_type=MESH,
            ).start()

    for load in loads:
        load.wait()
    pl.semaphore_wait(barrier, len(ORDER) + 2)

    lower = lax.broadcasted_iota(jnp.int32, (64, LANES), 1) < LANES // 2

    def pack(index, carry):
        top = pl.ds(pl.multiple_of(PAD + index * 64, 8), 64)
        bottom = pl.ds(pl.multiple_of(PAD + half + index * 64, 8), 64)
        packed = pl.ds(pl.multiple_of(index * 64, 64), 64)
        first, last = src[0, bottom], src[tiles - 1, bottom]
        pack_out[0, packed] = jnp.where(lower, src[0, top], pltpu.roll(first, LANES // 2, 1))
        pack_out[1, packed] = jnp.where(lower, pltpu.roll(last, LANES // 2, 1), src[tiles - 1, top])
        return carry

    lax.fori_loop(0, half // 64, pack, 0)
    halos = []
    for side, target in enumerate((left, right)):
        halo = pltpu.make_async_remote_copy(
            src_ref=pack_out.at[side],
            dst_ref=pack_in.at[side],
            send_sem=halo_send_sem.at[side],
            recv_sem=halo_recv_sem.at[side],
            device_id=(me, target),
            device_id_type=MESH,
        )
        halo.start()
        halos.append(halo)

    def inner(index, carry):
        send_piece(1 + index // parts, index % parts)
        return carry

    lax.fori_loop(0, 2 * parts, inner, 0)

    for halo in halos:
        halo.wait()

    has_left = x > 0
    has_right = x < 3

    def unpack(index, carry):
        top = pl.ds(pl.multiple_of(PAD + index * 64, 8), 64)
        bottom = pl.ds(pl.multiple_of(PAD + half + index * 64, 8), 64)
        packed = pl.ds(pl.multiple_of(index * 64, 64), 64)
        from_right = jnp.where(has_right, pack_in[0, packed], 0.0)
        from_left = jnp.where(has_left, pack_in[1, packed], 0.0)
        src[tiles, top] = jnp.where(lower, from_right, from_left)
        src[tiles, bottom] = pltpu.roll(jnp.where(lower, from_left, from_right), LANES // 2, 1)
        return carry

    lax.fori_loop(0, half // 64, unpack, 0)

    def outer(index, carry):
        send_piece((tiles - 1) * (index // parts), index % parts)
        return carry

    lax.fori_loop(0, 2 * parts, outer, 0)

    def keep(index, carry):
        for tile in range(tiles):
            piece = pl.ds(pl.multiple_of(index * PIECE, PIECE), PIECE)
            out_ref[me, piece, pl.ds(tile * LANES, LANES)] = blend(me, tile, index)
        return carry

    lax.fori_loop(0, parts, keep, 0)

    for slot, (dy, dz, dc) in enumerate(ORDER):
        source = member(dy, dz, dc, -1)
        pltpu.make_async_copy(send.at[slot], send.at[slot], send_sem.at[slot]).wait()
        pltpu.make_async_copy(out_ref.at[source], out_ref.at[source], recv_sem.at[slot]).wait()


def body(scenes, offset_y, offset_x, frac_y, frac_x):
    rows, cols = scenes.shape[1:]
    tiles = cols // LANES
    members = lax.axis_size("tm")
    tile_rows = rows // members
    smem = pl.BlockSpec(memory_space=pltpu.SMEM)
    return pl.pallas_call(
        warp_kernel,
        out_shape=jax.ShapeDtypeStruct((members, tile_rows, cols), jnp.float32),
        in_specs=[smem, smem, smem, smem, pl.BlockSpec(memory_space=pltpu.HBM)],
        out_specs=pl.BlockSpec(memory_space=pltpu.VMEM),
        scratch_shapes=[
            pltpu.VMEM((tiles + 1, rows + 2 * PAD, LANES), jnp.float32),
            pltpu.VMEM((len(ORDER), tiles, tile_rows, LANES), jnp.float32),
            pltpu.VMEM((2, rows // 2, LANES), jnp.float32),
            pltpu.VMEM((2, rows // 2, LANES), jnp.float32),
            pltpu.SemaphoreType.DMA((tiles,)),
            pltpu.SemaphoreType.DMA((len(ORDER),)),
            pltpu.SemaphoreType.DMA((len(ORDER),)),
            pltpu.SemaphoreType.DMA((2,)),
            pltpu.SemaphoreType.DMA((2,)),
        ],
        compiler_params=pltpu.CompilerParams(
            collective_id=0, has_side_effects=True, vmem_limit_bytes=48 << 20
        ),
    )(offset_y, offset_x, frac_y, frac_x, scenes)


def solution(mesh):
    return jax.shard_map(
        body,
        mesh=mesh,
        in_specs=(P("tm", None, "space"), P(), P(), P(), P()),
        out_specs=P(None, "tm", "space"),
        check_vma=False,
    )
```

time: 191 us -> 121 us (0.63)
  Pallas kernels: 0 us -> 109 us
  blocking collectives: 106 us -> 0 us
  other arithmetic: 39.3 us -> 0 us
  waiting for transfers between devices: 15.1 us -> 0 us
  local copies, waits for them, and re-layouts: 18.8 us -> 11 us
  starting transfers between devices: 6.27 us -> 0 us
  between operations: 5.32 us -> 0.01 us
    pallas_call x0 -> x1, Pallas kernels: none -> 109 us  [body(): pl.pallas_call(warp_kernel, out_shape=jax.ShapeDtypeStruct((members, tile...]
    all_to_all x1 -> x0, blocking collectives: 106 us -> none  [body(): lax.all_to_all(row_warped, 'tm', split_axis=1, concat_axis=0, tiled=True)]
    add x2 -> x0, other arithmetic: 28 us -> none  [the longest x1 15.4 us: blend_scene(): return weight_col * before_pixel + (1.0 - weight_col) * at_pixel]
    ppermute x2 -> x0, waiting for transfers between devices: 15.1 us -> none  [the longest x1 10.2 us: with_halo(): lax.ppermute(lax.slice_in_dim(block, block.shape[dim] - width, None, axis...]
    concatenate x1 -> x0, other arithmetic: 11.3 us -> none  [with_halo(): block = jnp.concatenate([low, block, high], axis=dim)]
    ppermute x2 -> x0, starting transfers between devices: 6.27 us -> none  [the longest x1 4.99 us: with_halo(): lax.ppermute(lax.slice_in_dim(block, block.shape[dim] - width, None, axis...]
    ppermute x2 -> x0, local copies, waits for them, and re-layouts: 4.97 us -> none  [the longest x1 3.15 us: with_halo(): lax.ppermute(lax.slice_in_dim(block, 0, width, axis=dim), axis, backward)]
    slice x1 -> x0, local copies, waits for them, and re-layouts: 4.23 us -> none  [with_halo(): lax.slice_in_dim(block, block.shape[dim] - width, None, axis=dim)]
  transfers between devices with their start and end apart: 2 -> 0, of which waited for: 2 -> 0; matrix products, arithmetic and copies ran while one was open for 3% -> 0% of each run, Pallas kernels for 0% -> 0%
where the time goes in v1:
time: 121 us; the launch traced here: 120 us
  Pallas kernels  109 us (90%)
  local copies, waits for them, and re-layouts  11 us (9%)
    pallas_call x1, Pallas kernels, body(): pl.pallas_call(warp_kernel, out_shape=jax.ShapeDtypeStruct((members, tile...  109 us
    unnamed x9, local copies, waits for them, and re-layouts  11 us

profile of v1, /device:TPU:1, one launch (start us, length us, event | category | flops | bytes accessed | tf_op | source)
XLA Modules:
  0.0 120.3 jit_solution(17745753937647826633)
XLA Ops:
  0.0 0.0 copy-start
  0.0 0.7 copy-done
  0.7 0.0 copy-start.1
  0.7 0.7 copy-done.1
  1.3 0.0 copy-start.2
  1.3 0.7 copy-done.2
  2.0 0.0 copy-start.3
  2.0 0.7 copy-done.3
  2.6 109.3 %shard_map.55 = f32[32,128,512]{2,1,0:T(8,128)} custom-call(s32[32]{0:T(128)S(1)} %copy-done, s32[32]{0:T(128)S(1)} %copy-done.1, f32[32]{0:T(128)S(1)} %copy-done.2, f32[32]{0:T(128)S(1)} %copy-done.3, f32[1,4096,512]{2,1,0:T(8,128)} %scene_ref.1), custom_call_target="tpu_custom_call" | custom-call | tf_op jit(solution)/shard_map/pallas_call | solution.py:196
  112.0 8.4 %copy.7 = f32[32,128,512]{2,1,0:T(8,128)} copy(f32[32,128,512]{2,1,0:T(8,128)} %shard_map.55) | data formatting | bytes 16777216
Async XLA Ops:
  0.0 0.7 copy-start
  0.7 0.7 copy-start.1
  1.3 0.7 copy-start.2
  2.0 0.7 copy-start.3

commit v2 on v1

--- a/solution.py
+++ b/solution.py
@@ -8,7 +8,7 @@
 MESH = pl.DeviceIdType.MESH
 LANES = 128
 PAD = 136
-PIECE = 32
+PIECE = 64
 
 
 def send_order():
@@ -28,8 +28,9 @@
 
 
 def warp_kernel(
-    oy_ref, ox_ref, fy_ref, fx_ref, scene_ref, out_ref,
-    src, send, pack_out, pack_in, load_sem, send_sem, recv_sem, halo_send_sem, halo_recv_sem,
+    oy_hbm, ox_hbm, fy_hbm, fx_hbm, scene_ref, out_ref,
+    oy_ref, ox_ref, fy_ref, fx_ref, src, send, pack_out, pack_in,
+    load_sem, param_sem, send_sem, recv_sem, halo_send_sem, halo_recv_sem,
 ):
     rows = scene_ref.shape[1]
     tiles = scene_ref.shape[2] // LANES
@@ -55,6 +56,11 @@
         pl.semaphore_signal(barrier, inc=1, device_id=(me, side), device_id_type=MESH)
 
     loads = []
+    params = ((oy_hbm, oy_ref), (ox_hbm, ox_ref), (fy_hbm, fy_ref), (fx_hbm, fx_ref))
+    for index, (hbm, smem) in enumerate(params):
+        load = pltpu.make_async_copy(hbm, smem, param_sem.at[index])
+        load.start()
+        loads.append(load)
     for tile in range(tiles):
         load = pltpu.make_async_copy(
             scene_ref.at[0, :, pl.ds(tile * LANES, LANES)],
@@ -67,6 +73,9 @@
     for plane in range(tiles + 1):
         src[plane, pl.ds(0, PAD)] = zero_rows
         src[plane, pl.ds(PAD + rows, PAD)] = zero_rows
+
+    for load in loads:
+        load.wait()
 
     shift_y, shift_x = oy_ref[me], ox_ref[me]
     weight_y, weight_x = fy_ref[me], fx_ref[me]
@@ -114,8 +123,6 @@
                 device_id_type=MESH,
             ).start()
 
-    for load in loads:
-        load.wait()
     pl.semaphore_wait(barrier, len(ORDER) + 2)
 
     lower = lax.broadcasted_iota(jnp.int32, (64, LANES), 1) < LANES // 2
@@ -129,10 +136,8 @@
         pack_out[1, packed] = jnp.where(lower, pltpu.roll(last, LANES // 2, 1), src[tiles - 1, top])
         return carry
 
-    lax.fori_loop(0, half // 64, pack, 0)
-    halos = []
-    for side, target in enumerate((left, right)):
-        halo = pltpu.make_async_remote_copy(
+    halos = [
+        pltpu.make_async_remote_copy(
             src_ref=pack_out.at[side],
             dst_ref=pack_in.at[side],
             send_sem=halo_send_sem.at[side],
@@ -140,11 +145,18 @@
             device_id=(me, target),
             device_id_type=MESH,
         )
-        halo.start()
-        halos.append(halo)
+        for side, target in enumerate((left, right))
+    ]
 
     def inner(index, carry):
         send_piece(1 + index // parts, index % parts)
+
+        @pl.when(index == 0)
+        def _():
+            lax.fori_loop(0, half // 64, pack, 0)
+            for halo in halos:
+                halo.start()
+
         return carry
 
     lax.fori_loop(0, 2 * parts, inner, 0)
@@ -192,27 +204,31 @@
     tiles = cols // LANES
     members = lax.axis_size("tm")
     tile_rows = rows // members
-    smem = pl.BlockSpec(memory_space=pltpu.SMEM)
     return pl.pallas_call(
         warp_kernel,
         out_shape=jax.ShapeDtypeStruct((members, tile_rows, cols), jnp.float32),
-        in_specs=[smem, smem, smem, smem, pl.BlockSpec(memory_space=pltpu.HBM)],
+        in_specs=[pl.BlockSpec(memory_space=pltpu.HBM)] * 5,
         out_specs=pl.BlockSpec(memory_space=pltpu.VMEM),
         scratch_shapes=[
+            pltpu.SMEM(offset_y.shape, jnp.int32),
+            pltpu.SMEM(offset_x.shape, jnp.int32),
+            pltpu.SMEM(frac_y.shape, jnp.float32),
+            pltpu.SMEM(frac_x.shape, jnp.float32),
             pltpu.VMEM((tiles + 1, rows + 2 * PAD, LANES), jnp.float32),
             pltpu.VMEM((len(ORDER), tiles, tile_rows, LANES), jnp.float32),
             pltpu.VMEM((2, rows // 2, LANES), jnp.float32),
             pltpu.VMEM((2, rows // 2, LANES), jnp.float32),
             pltpu.SemaphoreType.DMA((tiles,)),
+            pltpu.SemaphoreType.DMA((4,)),
             pltpu.SemaphoreType.DMA((len(ORDER),)),
             pltpu.SemaphoreType.DMA((len(ORDER),)),
             pltpu.SemaphoreType.DMA((2,)),
             pltpu.SemaphoreType.DMA((2,)),
         ],
         compiler_params=pltpu.CompilerParams(
-            collective_id=0, has_side_effects=True, vmem_limit_bytes=48 << 20
+            collective_id=0, has_side_effects=True, vmem_limit_bytes=28 << 20
         ),
-    )(offset_y, offset_x, frac_y, frac_x, scenes)
+    )(*[pltpu.with_memory_space_constraint(v, pltpu.HBM) for v in (offset_y, offset_x, frac_y, frac_x, scenes)])
 
 
 def solution(mesh):

time: 121 us -> 106 us (0.88)
  local copies, waits for them, and re-layouts: 11 us -> 3.4 us
  Pallas kernels: 109 us -> 102 us
    unnamed x9 -> x1, local copies, waits for them, and re-layouts: 11 us -> 3.4 us
    pallas_call x1, Pallas kernels: 109 us -> 102 us  [body(): pl.pallas_call(warp_kernel, out_shape=jax.ShapeDtypeStruct((members, tile...]
where the time goes in v2:
time: 106 us
  Pallas kernels  102 us (96%)
  local copies, waits for them, and re-layouts  3.4 us (3%)
    pallas_call x1, Pallas kernels, body(): pl.pallas_call(warp_kernel, out_shape=jax.ShapeDtypeStruct((members, tile...  102 us
    unnamed x1, local copies, waits for them, and re-layouts  3.4 us

profile of v2, /device:TPU:1, one launch (start us, length us, event | category | flops | bytes accessed | tf_op | source)
XLA Modules:
  0.0 105.8 jit_solution(11427426755936697616)
XLA Ops:
  0.0 102.4 %shard_map.55 = f32[32,128,512]{2,1,0:T(8,128)S(1)} custom-call(s32[32]{0:T(128)} %oy_hbm.1, s32[32]{0:T(128)} %ox_hbm.1, f32[32]{0:T(128)} %fy_hbm.1, f32[32]{0:T(128)} %fx_hbm.1, f32[1,4096,512]{2,1,0:T(8,128)} %scene_ref.1), custom_call_target="tpu_custom_call" | custom-call | tf_op jit(solution)/shard_map/pallas_call | solution.py:207
  102.4 3.4 %copy.7 = f32[32,128,512]{2,1,0:T(8,128)} copy(f32[32,128,512]{2,1,0:T(8,128)S(1)} %shard_map.55) | data formatting | bytes 16777216

commit v3 on v2

v3 whole, which is shorter than its diff:
```python
import jax
import jax.numpy as jnp
from jax import lax
from jax.experimental import pallas as pl
from jax.experimental.pallas import tpu as pltpu
from jax.sharding import PartitionSpec as P

MESH = pl.DeviceIdType.MESH
LANES = 128
PAD = 136
PIECE = 64


NEAR = ((1, 0), (3, 0), (0, 1), (0, 3))
FAR = (
    (2, 2), (2, 1), (1, 2), (2, 3), (3, 2), (2, 0), (0, 2), (1, 1), (3, 3), (1, 3), (3, 1),
)
CHIPS = NEAR + FAR
PEERS = 2 * len(CHIPS) + 1


def warp_kernel(
    oy_hbm, ox_hbm, fy_hbm, fx_hbm, scene_ref, out_ref,
    oy_ref, ox_ref, fy_ref, fx_ref, first, last, send, pack_out, pack_in,
    load_sem, param_sem, send_sem, recv_sem, halo_send_sem, halo_recv_sem,
):
    rows = scene_ref.shape[1]
    tiles = scene_ref.shape[2] // LANES
    tile_rows = out_ref.shape[1]
    half = rows // 2
    me = lax.axis_index("tm")
    x = lax.axis_index("space")
    y, z, core = me // 8, (me // 2) % 4, me % 2

    def member(chip, other, sign):
        dy, dz = chip
        return ((y + sign * dy + 4) % 4) * 8 + ((z + sign * dz + 4) % 4) * 2 + (core + other) % 2

    left, right = (x + 3) % 4, (x + 1) % 4
    here = (0, 0)

    planes = [first.at[0], first.at[1], first.at[2], last.at[0], last.at[1]]
    params = ((oy_hbm, oy_ref), (ox_hbm, ox_ref), (fy_hbm, fy_ref), (fx_hbm, fx_ref))
    loads = []
    for index, (hbm, smem) in enumerate(params):
        load = pltpu.make_async_copy(hbm, smem, param_sem.at[index])
        load.start()
        loads.append(load)
    for tile in range(tiles):
        load = pltpu.make_async_copy(
            scene_ref.at[0, :, pl.ds(tile * LANES, LANES)],
            planes[tile].at[pl.ds(PAD, rows)],
            load_sem.at[tile],
        )
        load.start()
        loads.append(load)

    barrier = pltpu.get_barrier_semaphore()
    for chip in FAR + NEAR:
        for other in range(2):
            pl.semaphore_signal(
                barrier, inc=1, device_id=(member(chip, other, -1), x), device_id_type=MESH
            )
    pl.semaphore_signal(barrier, inc=1, device_id=(member(here, 1, -1), x), device_id_type=MESH)
    for side in (left, right):
        pl.semaphore_signal(barrier, inc=1, device_id=(me, side), device_id_type=MESH)

    zero_rows = jnp.zeros((PAD, LANES), jnp.float32)
    for plane in planes:
        plane[pl.ds(0, PAD)] = zero_rows
        plane[pl.ds(PAD + rows, PAD)] = zero_rows

    for load in loads[:-1]:
        load.wait()

    shift_y, shift_x = oy_ref[me], ox_ref[me]
    weight_y, weight_x = fy_ref[me], fx_ref[me]
    lane = lax.broadcasted_iota(jnp.int32, (PIECE, LANES), 1)
    rightward = shift_x >= 0
    low = jnp.where(rightward, 0, -shift_x)
    high = jnp.where(rightward, LANES - shift_x, LANES)
    low_before = jnp.where(rightward, 0, -shift_x - 1)
    high_before = jnp.where(rightward, LANES - 1 - shift_x, LANES)
    own_at = (lane >= low) & (lane < high)
    own_before = (lane >= low_before) & (lane < high_before)
    roll_at = (shift_x + LANES) % LANES
    roll_before = (shift_x + 1 + LANES) % LANES

    def blend(dest, tile, part):
        base = jnp.clip(dest * tile_rows - shift_y - 1, -tile_rows - 1, rows)
        base = base + (PAD + part * PIECE)

        def blend_rows(read):
            above = read(pl.ds(base, PIECE))
            at = read(pl.ds(base + 1, PIECE))
            return weight_y * above + (1.0 - weight_y) * at

        own = blend_rows(lambda at: planes[tile][at])
        if tile == 1:
            side = jnp.where(rightward, 0, 2)
            beside = blend_rows(lambda at: first[side, at])
        else:
            before, after = planes[(tile - 1) % (tiles + 1)], planes[tile + 1]
            beside = blend_rows(lambda at: jnp.where(rightward, before[at], after[at]))
        at = pltpu.roll(jnp.where(own_at, own, beside), roll_at, 1)
        before = pltpu.roll(jnp.where(own_before, own, beside), roll_before, 1)
        return weight_x * before + (1.0 - weight_x) * at

    parts = tile_rows // PIECE

    def send_piece(slot, dest, tile, part):
        piece = pl.ds(pl.multiple_of(part * PIECE, PIECE), PIECE)
        send[slot, tile, piece] = blend(dest, tile, part)
        pltpu.make_async_remote_copy(
            src_ref=send.at[slot, tile, piece],
            dst_ref=out_ref.at[me, piece, pl.ds(tile * LANES, LANES)],
            send_sem=send_sem.at[slot],
            recv_sem=recv_sem.at[slot],
            device_id=(dest, x),
            device_id_type=MESH,
        ).start()

    def send_tile(chips, tile):
        def step(index, carry):
            part, other = index // 2, index % 2
            for chip in chips:
                slot = 2 * CHIPS.index(chip) + other
                send_piece(slot, member(chip, other, 1), tile, part)
            return carry

        lax.fori_loop(0, 2 * parts, step, 0)

    pl.semaphore_wait(barrier, PEERS + 2)

    send_tile(NEAR, 1)
    loads[-1].wait()

    lower = lax.broadcasted_iota(jnp.int32, (64, LANES), 1) < LANES // 2

    def pack(index, carry):
        top = pl.ds(pl.multiple_of(PAD + index * 64, 8), 64)
        bottom = pl.ds(pl.multiple_of(PAD + half + index * 64, 8), 64)
        packed = pl.ds(pl.multiple_of(index * 64, 64), 64)
        low_edge, high_edge = planes[0], planes[tiles - 1]
        pack_out[0, packed] = jnp.where(
            lower, low_edge[top], pltpu.roll(low_edge[bottom], LANES // 2, 1)
        )
        pack_out[1, packed] = jnp.where(
            lower, pltpu.roll(high_edge[bottom], LANES // 2, 1), high_edge[top]
        )
        return carry

    halos = [
        pltpu.make_async_remote_copy(
            src_ref=pack_out.at[side],
            dst_ref=pack_in.at[side],
            send_sem=halo_send_sem.at[side],
            recv_sem=halo_recv_sem.at[side],
            device_id=(me, target),
            device_id_type=MESH,
        )
        for side, target in enumerate((left, right))
    ]

    send_tile(FAR, 1)
    lax.fori_loop(0, half // 64, pack, 0)
    for halo in halos:
        halo.start()

    send_tile(CHIPS, 2)

    for halo in halos:
        halo.wait()

    has_left = x > 0
    has_right = x < 3

    def unpack(index, carry):
        top = pl.ds(pl.multiple_of(PAD + index * 64, 8), 64)
        bottom = pl.ds(pl.multiple_of(PAD + half + index * 64, 8), 64)
        packed = pl.ds(pl.multiple_of(index * 64, 64), 64)
        from_right = jnp.where(has_right, pack_in[0, packed], 0.0)
        from_left = jnp.where(has_left, pack_in[1, packed], 0.0)
        planes[tiles][top] = jnp.where(lower, from_right, from_left)
        planes[tiles][bottom] = pltpu.roll(jnp.where(lower, from_left, from_right), LANES // 2, 1)
        return carry

    lax.fori_loop(0, half // 64, unpack, 0)

    send_tile(CHIPS, 0)
    send_tile(FAR, 3)

    def across(part, carry):
        for tile in range(tiles):
            send_piece(PEERS - 1, member(here, 1, 1), tile, part)
        return carry

    lax.fori_loop(0, parts, across, 0)

    for tile in (3,):
        send_tile(NEAR, tile)

    def keep(part, carry):
        for tile in range(tiles):
            piece = pl.ds(pl.multiple_of(part * PIECE, PIECE), PIECE)
            out_ref[me, piece, pl.ds(tile * LANES, LANES)] = blend(me, tile, part)
        return carry

    lax.fori_loop(0, parts, keep, 0)

    for slot in range(PEERS):
        chip, other = (here, 1) if slot == PEERS - 1 else (CHIPS[slot // 2], slot % 2)
        source = member(chip, other, -1)
        pltpu.make_async_copy(send.at[slot], send.at[slot], send_sem.at[slot]).wait()
        pltpu.make_async_copy(out_ref.at[source], out_ref.at[source], recv_sem.at[slot]).wait()


def body(scenes, offset_y, offset_x, frac_y, frac_x):
    rows, cols = scenes.shape[1:]
    tiles = cols // LANES
    members = lax.axis_size("tm")
    tile_rows = rows // members
    return pl.pallas_call(
        warp_kernel,
        out_shape=jax.ShapeDtypeStruct((members, tile_rows, cols), jnp.float32),
        in_specs=[pl.BlockSpec(memory_space=pltpu.HBM)] * 5,
        out_specs=pl.BlockSpec(memory_space=pltpu.VMEM),
        scratch_shapes=[
            pltpu.SMEM(offset_y.shape, jnp.int32),
            pltpu.SMEM(offset_x.shape, jnp.int32),
            pltpu.SMEM(frac_y.shape, jnp.float32),
            pltpu.SMEM(frac_x.shape, jnp.float32),
            pltpu.VMEM((3, rows + 2 * PAD, LANES), jnp.float32),
            pltpu.VMEM((2, rows + 2 * PAD, LANES), jnp.float32),
            pltpu.VMEM((PEERS, tiles, tile_rows, LANES), jnp.float32),
            pltpu.VMEM((2, rows // 2, LANES), jnp.float32),
            pltpu.VMEM((2, rows // 2, LANES), jnp.float32),
            pltpu.SemaphoreType.DMA((tiles,)),
            pltpu.SemaphoreType.DMA((4,)),
            pltpu.SemaphoreType.DMA((PEERS,)),
            pltpu.SemaphoreType.DMA((PEERS,)),
            pltpu.SemaphoreType.DMA((2,)),
            pltpu.SemaphoreType.DMA((2,)),
        ],
        compiler_params=pltpu.CompilerParams(
            collective_id=0, has_side_effects=True, vmem_limit_bytes=28 << 20
        ),
    )(*[pltpu.with_memory_space_constraint(v, pltpu.HBM) for v in (offset_y, offset_x, frac_y, frac_x, scenes)])


def solution(mesh):
    return jax.shard_map(
        body,
        mesh=mesh,
        in_specs=(P("tm", None, "space"), P(), P(), P(), P()),
        out_specs=P(None, "tm", "space"),
        check_vma=False,
    )
```

time: 106 us -> 105 us (level)
    pallas_call x1, Pallas kernels: 102 us -> 101 us  [body(): pl.pallas_call(warp_kernel, out_shape=jax.ShapeDtypeStruct((members, tile...]
where the time goes in v3:
time: 105 us
  Pallas kernels  101 us (96%)
  local copies, waits for them, and re-layouts  3.4 us (3%)
    pallas_call x1, Pallas kernels, body(): pl.pallas_call(warp_kernel, out_shape=jax.ShapeDtypeStruct((members, tile...  101 us
    unnamed x1, local copies, waits for them, and re-layouts  3.4 us

profile of v3, /device:TPU:1, one launch (start us, length us, event | category | flops | bytes accessed | tf_op | source)
XLA Modules:
  0.0 104.6 jit_solution(2542964402947490742)
XLA Ops:
  0.0 101.2 %shard_map.55 = f32[32,128,512]{2,1,0:T(8,128)S(1)} custom-call(s32[32]{0:T(128)} %oy_hbm.1, s32[32]{0:T(128)} %ox_hbm.1, f32[32]{0:T(128)} %fy_hbm.1, f32[32]{0:T(128)} %fx_hbm.1, f32[1,4096,512]{2,1,0:T(8,128)} %scene_ref.1), custom_call_target="tpu_custom_call" | custom-call | tf_op jit(solution)/shard_map/pallas_call | solution.py:223
  101.2 3.4 %copy.7 = f32[32,128,512]{2,1,0:T(8,128)} copy(f32[32,128,512]{2,1,0:T(8,128)S(1)} %shard_map.55) | data formatting | bytes 16777216

commit v4 on v3

--- a/solution.py
+++ b/solution.py
@@ -114,8 +114,8 @@
         pltpu.make_async_remote_copy(
             src_ref=send.at[slot, tile, piece],
             dst_ref=out_ref.at[me, piece, pl.ds(tile * LANES, LANES)],
-            send_sem=send_sem.at[slot],
-            recv_sem=recv_sem.at[slot],
+            send_sem=send_sem,
+            recv_sem=recv_sem,
             device_id=(dest, x),
             device_id_type=MESH,
         ).start()
@@ -208,11 +208,8 @@
 
     lax.fori_loop(0, parts, keep, 0)
 
-    for slot in range(PEERS):
-        chip, other = (here, 1) if slot == PEERS - 1 else (CHIPS[slot // 2], slot % 2)
-        source = member(chip, other, -1)
-        pltpu.make_async_copy(send.at[slot], send.at[slot], send_sem.at[slot]).wait()
-        pltpu.make_async_copy(out_ref.at[source], out_ref.at[source], recv_sem.at[slot]).wait()
+    pltpu.make_async_copy(send, send, send_sem).wait()
+    pltpu.make_async_copy(send, send, recv_sem).wait()
 
 
 def body(scenes, offset_y, offset_x, frac_y, frac_x):
@@ -237,8 +234,8 @@
             pltpu.VMEM((2, rows // 2, LANES), jnp.float32),
             pltpu.SemaphoreType.DMA((tiles,)),
             pltpu.SemaphoreType.DMA((4,)),
-            pltpu.SemaphoreType.DMA((PEERS,)),
-            pltpu.SemaphoreType.DMA((PEERS,)),
+            pltpu.SemaphoreType.DMA(()),
+            pltpu.SemaphoreType.DMA(()),
             pltpu.SemaphoreType.DMA((2,)),
             pltpu.SemaphoreType.DMA((2,)),
         ],

time: 105 us -> 104 us (level)
  no operation moved by 1% of the time
where the time goes in v4:
time: 104 us
  Pallas kernels  101 us (97%)
  local copies, waits for them, and re-layouts  3.4 us (3%)
    pallas_call x1, Pallas kernels, body(): pl.pallas_call(warp_kernel, out_shape=jax.ShapeDtypeStruct((members, tile...  101 us
    unnamed x1, local copies, waits for them, and re-layouts  3.4 us

profile of v4, /device:TPU:1, one launch (start us, length us, event | category | flops | bytes accessed | tf_op | source)
XLA Modules:
  0.0 104.0 jit_solution(13264300925245420436)
XLA Ops:
  0.0 100.6 %shard_map.55 = f32[32,128,512]{2,1,0:T(8,128)S(1)} custom-call(s32[32]{0:T(128)} %oy_hbm.1, s32[32]{0:T(128)} %ox_hbm.1, f32[32]{0:T(128)} %fy_hbm.1, f32[32]{0:T(128)} %fx_hbm.1, f32[1,4096,512]{2,1,0:T(8,128)} %scene_ref.1), custom_call_target="tpu_custom_call" | custom-call | tf_op jit(solution)/shard_map/pallas_call | solution.py:220
  100.6 3.4 %copy.7 = f32[32,128,512]{2,1,0:T(8,128)} copy(f32[32,128,512]{2,1,0:T(8,128)S(1)} %shard_map.55) | data formatting | bytes 16777216

commit v5 on v4

--- a/solution.py
+++ b/solution.py
@@ -22,7 +22,7 @@
 def warp_kernel(
     oy_hbm, ox_hbm, fy_hbm, fx_hbm, scene_ref, out_ref,
     oy_ref, ox_ref, fy_ref, fx_ref, first, last, send, pack_out, pack_in,
-    load_sem, param_sem, send_sem, recv_sem, halo_send_sem, halo_recv_sem,
+    load_sem, param_sem, send_sem, recv_sem, halo_send_sem, halo_recv_sem, line_sem,
 ):
     rows = scene_ref.shape[1]
     tiles = scene_ref.shape[2] // LANES
@@ -56,7 +56,9 @@
         loads.append(load)
 
     barrier = pltpu.get_barrier_semaphore()
-    for chip in FAR + NEAR:
+    along_y = tuple((dy, 0) for dy in (2, 1, 3))
+    along_z = tuple((0, dz) for dz in (2, 1, 3))
+    for chip in along_y + along_z:
         for other in range(2):
             pl.semaphore_signal(
                 barrier, inc=1, device_id=(member(chip, other, -1), x), device_id_type=MESH
@@ -70,6 +72,11 @@
         plane[pl.ds(0, PAD)] = zero_rows
         plane[pl.ds(PAD + rows, PAD)] = zero_rows
 
+    pl.semaphore_wait(barrier, 2 * len(along_y + along_z) + 3)
+    for chip in along_z:
+        pl.semaphore_signal(
+            line_sem, inc=1, device_id=(member(chip, 0, -1), x), device_id_type=MESH
+        )
     for load in loads[:-1]:
         load.wait()
 
@@ -130,9 +137,8 @@
 
         lax.fori_loop(0, 2 * parts, step, 0)
 
-    pl.semaphore_wait(barrier, PEERS + 2)
-
     send_tile(NEAR, 1)
+    pl.semaphore_wait(line_sem, len(along_z))
     loads[-1].wait()
 
     lower = lax.broadcasted_iota(jnp.int32, (64, LANES), 1) < LANES // 2
@@ -163,11 +169,10 @@
     ]
 
     send_tile(FAR, 1)
+    send_tile(CHIPS, 2)
     lax.fori_loop(0, half // 64, pack, 0)
     for halo in halos:
         halo.start()
-
-    send_tile(CHIPS, 2)
 
     for halo in halos:
         halo.wait()
@@ -238,6 +243,7 @@
             pltpu.SemaphoreType.DMA(()),
             pltpu.SemaphoreType.DMA((2,)),
             pltpu.SemaphoreType.DMA((2,)),
+            pltpu.SemaphoreType.REGULAR,
         ],
         compiler_params=pltpu.CompilerParams(
             collective_id=0, has_side_effects=True, vmem_limit_bytes=28 << 20

time: 104 us -> 103 us (level)
  Pallas kernels: 101 us -> 99.7 us
where the time goes in v5:
time: 103 us
  Pallas kernels  99.7 us (97%)
  local copies, waits for them, and re-layouts  3.4 us (3%)
    pallas_call x1, Pallas kernels, body(): pl.pallas_call(warp_kernel, out_shape=jax.ShapeDtypeStruct((members, tile...  99.7 us
    unnamed x1, local copies, waits for them, and re-layouts  3.4 us

profile of v5, /device:TPU:1, one launch (start us, length us, event | category | flops | bytes accessed | tf_op | source)
XLA Modules:
  0.0 103.1 jit_solution(16555494383882547380)
XLA Ops:
  0.0 99.7 %shard_map.55 = f32[32,128,512]{2,1,0:T(8,128)S(1)} custom-call(s32[32]{0:T(128)} %oy_hbm.1, s32[32]{0:T(128)} %ox_hbm.1, f32[32]{0:T(128)} %fy_hbm.1, f32[32]{0:T(128)} %fx_hbm.1, f32[1,4096,512]{2,1,0:T(8,128)} %scene_ref.1), custom_call_target="tpu_custom_call" | custom-call | tf_op jit(solution)/shard_map/pallas_call | solution.py:225
  99.7 3.4 %copy.7 = f32[32,128,512]{2,1,0:T(8,128)} copy(f32[32,128,512]{2,1,0:T(8,128)S(1)} %shard_map.55) | data formatting | bytes 16777216

commit v6 on v5

--- a/solution.py
+++ b/solution.py
@@ -129,7 +129,7 @@
 
     def send_tile(chips, tile):
         def step(index, carry):
-            part, other = index // 2, index % 2
+            part, other = index % parts, (index // parts + core) % 2
             for chip in chips:
                 slot = 2 * CHIPS.index(chip) + other
                 send_piece(slot, member(chip, other, 1), tile, part)
@@ -246,7 +246,7 @@
             pltpu.SemaphoreType.REGULAR,
         ],
         compiler_params=pltpu.CompilerParams(
-            collective_id=0, has_side_effects=True, vmem_limit_bytes=28 << 20
+            collective_id=0, has_side_effects=True, vmem_limit_bytes=36 << 20
         ),
     )(*[pltpu.with_memory_space_constraint(v, pltpu.HBM) for v in (offset_y, offset_x, frac_y, frac_x, scenes)])
 

time: 103 us -> 103 us (level)
  no operation moved by 1% of the time
where the time goes in v6:
time: 103 us
  Pallas kernels  99.6 us (97%)
  local copies, waits for them, and re-layouts  3.4 us (3%)
    pallas_call x1, Pallas kernels, body(): pl.pallas_call(warp_kernel, out_shape=jax.ShapeDtypeStruct((members, tile...  99.6 us
    unnamed x1, local copies, waits for them, and re-layouts  3.4 us

profile of v6, /device:TPU:1, one launch (start us, length us, event | category | flops | bytes accessed | tf_op | source)
XLA Modules:
  0.0 103.0 jit_solution(15691752402839120765)
XLA Ops:
  0.0 99.6 %shard_map.55 = f32[32,128,512]{2,1,0:T(8,128)S(1)} custom-call(s32[32]{0:T(128)} %oy_hbm.1, s32[32]{0:T(128)} %ox_hbm.1, f32[32]{0:T(128)} %fy_hbm.1, f32[32]{0:T(128)} %fx_hbm.1, f32[1,4096,512]{2,1,0:T(8,128)} %scene_ref.1), custom_call_target="tpu_custom_call" | custom-call | tf_op jit(solution)/shard_map/pallas_call | solution.py:225
  99.6 3.4 %copy.7 = f32[32,128,512]{2,1,0:T(8,128)} copy(f32[32,128,512]{2,1,0:T(8,128)S(1)} %shard_map.55) | data formatting | bytes 16777216

commit v7 on v6

--- a/solution.py
+++ b/solution.py
@@ -9,6 +9,7 @@
 LANES = 128
 PAD = 136
 PIECE = 64
+HEAD = 128
 
 
 NEAR = ((1, 0), (3, 0), (0, 1), (0, 3))
@@ -82,7 +83,7 @@
 
     shift_y, shift_x = oy_ref[me], ox_ref[me]
     weight_y, weight_x = fy_ref[me], fx_ref[me]
-    lane = lax.broadcasted_iota(jnp.int32, (PIECE, LANES), 1)
+    lane = lax.broadcasted_iota(jnp.int32, (1, LANES), 1)
     rightward = shift_x >= 0
     low = jnp.where(rightward, 0, -shift_x)
     high = jnp.where(rightward, LANES - shift_x, LANES)
@@ -93,13 +94,13 @@
     roll_at = (shift_x + LANES) % LANES
     roll_before = (shift_x + 1 + LANES) % LANES
 
-    def blend(dest, tile, part):
+    def blend(dest, tile, part, size=PIECE):
         base = jnp.clip(dest * tile_rows - shift_y - 1, -tile_rows - 1, rows)
-        base = base + (PAD + part * PIECE)
+        base = base + (PAD + part * size)
 
         def blend_rows(read):
-            above = read(pl.ds(base, PIECE))
-            at = read(pl.ds(base + 1, PIECE))
+            above = read(pl.ds(base, size))
+            at = read(pl.ds(base + 1, size))
             return weight_y * above + (1.0 - weight_y) * at
 
         own = blend_rows(lambda at: planes[tile][at])
@@ -109,15 +110,15 @@
         else:
             before, after = planes[(tile - 1) % (tiles + 1)], planes[tile + 1]
             beside = blend_rows(lambda at: jnp.where(rightward, before[at], after[at]))
-        at = pltpu.roll(jnp.where(own_at, own, beside), roll_at, 1)
-        before = pltpu.roll(jnp.where(own_before, own, beside), roll_before, 1)
+        at = pltpu.roll(jnp.where(jnp.broadcast_to(own_at, own.shape), own, beside), roll_at, 1)
+        before = pltpu.roll(jnp.where(jnp.broadcast_to(own_before, own.shape), own, beside), roll_before, 1)
         return weight_x * before + (1.0 - weight_x) * at
 
     parts = tile_rows // PIECE
 
-    def send_piece(slot, dest, tile, part):
-        piece = pl.ds(pl.multiple_of(part * PIECE, PIECE), PIECE)
-        send[slot, tile, piece] = blend(dest, tile, part)
+    def send_piece(slot, dest, tile, part, size=PIECE):
+        piece = pl.ds(pl.multiple_of(part * size, size), size)
+        send[slot, tile, piece] = blend(dest, tile, part, size)
         pltpu.make_async_remote_copy(
             src_ref=send.at[slot, tile, piece],
             dst_ref=out_ref.at[me, piece, pl.ds(tile * LANES, LANES)],
@@ -127,17 +128,19 @@
             device_id_type=MESH,
         ).start()
 
-    def send_tile(chips, tile):
+    def send_tile(chips, tile, size=PIECE):
+        parts = tile_rows // size
+
         def step(index, carry):
             part, other = index % parts, (index // parts + core) % 2
             for chip in chips:
                 slot = 2 * CHIPS.index(chip) + other
-                send_piece(slot, member(chip, other, 1), tile, part)
+                send_piece(slot, member(chip, other, 1), tile, part, size)
             return carry
 
         lax.fori_loop(0, 2 * parts, step, 0)
 
-    send_tile(NEAR, 1)
+    send_tile(NEAR, 1, HEAD)
     pl.semaphore_wait(line_sem, len(along_z))
     loads[-1].wait()
 

time: 103 us -> 103 us (level)
  no operation moved by 1% of the time
where the time goes in v7:
time: 103 us
  Pallas kernels  99.5 us (97%)
  local copies, waits for them, and re-layouts  3.4 us (3%)
    pallas_call x1, Pallas kernels, body(): pl.pallas_call(warp_kernel, out_shape=jax.ShapeDtypeStruct((members, tile...  99.5 us
    unnamed x1, local copies, waits for them, and re-layouts  3.4 us

profile of v7, /device:TPU:1, one launch (start us, length us, event | category | flops | bytes accessed | tf_op | source)
XLA Modules:
  0.0 102.9 jit_solution(17124454396106189759)
XLA Ops:
  0.0 99.5 %shard_map.55 = f32[32,128,512]{2,1,0:T(8,128)S(1)} custom-call(s32[32]{0:T(128)} %oy_hbm.1, s32[32]{0:T(128)} %ox_hbm.1, f32[32]{0:T(128)} %fy_hbm.1, f32[32]{0:T(128)} %fx_hbm.1, f32[1,4096,512]{2,1,0:T(8,128)} %scene_ref.1), custom_call_target="tpu_custom_call" | custom-call | tf_op jit(solution)/shard_map/pallas_call | solution.py:228
  99.5 3.4 %copy.7 = f32[32,128,512]{2,1,0:T(8,128)} copy(f32[32,128,512]{2,1,0:T(8,128)S(1)} %shard_map.55) | data formatting | bytes 16777216
